TPU v7x, 256 devices: a whole 4x4x8 slice. The times are simulated.
256 devices in a mesh: section: 2 (over core), req: 16 (over x, y), head: 8 (over z).
Axes of the slice: x: 4, y: 4, z: 8, core: 2. Of those that a mesh axis runs over, the one named last changes fastest.
Arguments:
- tokens: bfloat16 [256, 8192], P(None, 'req'), may hold values from -14 to 14
- attention_gain: bfloat16 [2, 8192], P('section', 'req'), may hold values from 0.099609375 to 1.8984375
- query_key_value_weight: bfloat16 [2, 8192, 8, 1280], P('section', 'req', 'head'), may hold values from -0.0625 to 0.0625
- head_output_weight: bfloat16 [2, 8, 1024, 8192], P('section', 'head', None, 'req'), may hold values from -0.0625 to 0.0625
- feedforward_gain: bfloat16 [2, 8192], P('section', 'req'), may hold values from 0.099609375 to 1.8984375
- gate_up: bfloat16 [2, 8192, 2, 14336], P('section', 'req', None, 'head'), may hold values from -0.0625 to 0.0625
- down_weight: bfloat16 [2, 14336, 8192], P('section', 'head', 'req'), may hold values from -0.046875 to 0.046875
- packed_cache: bfloat16 [2, 32768, 8, 256], P('section', 'req', 'head'), may hold values from -70 to 70
- long_cache: bfloat16 [2, 2, 32768, 8, 256], P('section', None, 'req', 'head'), may hold values from -70 to 70
- lengths: int32 [16, 16], P('req'), may hold values from 1 to 256, 2048 in all within a row
- long_split: int32 [2, 16], P(None, 'req'), may hold values from 1 to 2048, 16384 in all within a row
Outputs:
- layer_outputs: bfloat16 [2, 256, 8192], P('section', None, 'req')
Inputs may be any that keep to these rules, and one draw needn't show every extreme that they name: Row g holds the lengths of the 16 requests of request group g in order; they sum to 2048, and the requests' keys fill that group's 2048 slots of packed_cache one request after another. `long_split`: entry (j, g) counts the live slots, the first ones, of group g's 2048 slots of long request j; each row sums to 16384.
All inputs are finite; a program needn't handle non-finite values.
Results may differ from a plain program's by a relative error of at most 0.04.
Values may be sent and summed in bfloat16 or wider, within the bound.
A program may use at most 64 MiB of HBM per device.

v0:
```python
import math
import jax
import jax.numpy as jnp
from jax import lax
from jax.sharding import PartitionSpec as P

MODEL_WIDTH = 8192
QUERY_HEADS = 64
KEY_VALUE_HEADS = 8
HEAD_SIZE = 128
LONG = 16384
EPSILON = 1e-05


def merged(part, axis, combine):
    gathered = jax.tree.map(lambda a: lax.all_gather(a, axis), part)

    def take(source):
        return jax.tree.map(lambda a: lax.dynamic_index_in_dim(a, source, 0, False), gathered)

    return lax.fori_loop(
        1, lax.axis_size(axis), lambda source, state: combine(state, take(source)), take(0)
    )


def shifted(value, axis, by):
    peers = lax.axis_size(axis)
    pairs = [(i, i + by) for i in range(peers) if 0 <= i + by < peers]
    return lax.ppermute(value, axis, pairs)


def rotate(values, position):
    half_dim = values.shape[-1] // 2
    freq_ids = jnp.arange(half_dim).astype(jnp.float32)
    inverse = 1.0 / 10000.0 ** (freq_ids * 2.0 / values.shape[-1])
    angles = position.astype(jnp.float32)[:, None] * inverse[None, :]
    cosine = jnp.cos(angles)[:, None, None, :]
    sine_part = jnp.sin(angles)[:, None, None, :]
    lower_half = values[..., :half_dim]
    upper_half = values[..., half_dim:]
    return jnp.concatenate(
        [
            lower_half * cosine - upper_half * sine_part,
            upper_half * cosine + lower_half * sine_part,
        ],
        -1,
    )


def add_pair(earlier, second_part):
    return earlier + second_part


def combine_partial(earlier, second_part):
    peak = jnp.maximum(earlier[0], second_part[0])
    left_factor = jnp.exp(earlier[0] - peak)
    right_factor = jnp.exp(second_part[0] - peak)
    softmax_total = earlier[1] * left_factor + second_part[1] * right_factor
    weighted_sum = earlier[2] * left_factor[..., None] + second_part[2] * right_factor[..., None]
    return (peak, softmax_total, weighted_sum)


def over_requests(values, combiner):
    return merged(values, "req", combiner)


def rows_apply(values, row_fn):
    return row_fn(lax.all_gather(values, "req", axis=0, tiled=True), jnp.int32(0))


def rows_project(term_fn, row_count):
    return lax.psum_scatter(
        term_fn(jnp.int32(0), row_count * lax.axis_size("req")),
        "req",
        scatter_dimension=0,
        tiled=True,
    )


def head_total(values):
    return lax.psum(values, "head")


def keep_rows(piece_rows, start_row):
    return piece_rows


def norm_rows(values, gain_row):
    floats = values.astype(jnp.float32)
    squares = over_requests(jnp.sum(floats * floats, axis=-1), add_pair)
    return (
        floats * lax.rsqrt(squares / MODEL_WIDTH + EPSILON)[:, None] * gain_row.astype(jnp.float32)
    ).astype(jnp.bfloat16)


def decoder_layer(
    inputs,
    micro_batch,
    attention_gain,
    query_key_value_weight,
    head_output_weight,
    feedforward_gain,
    gate_up,
    down_weight,
    packed_cache,
    long_cache,
    lengths,
    long_split,
):
    req_count = lax.axis_size("req")
    group_index = lax.axis_index("req")
    blocks = inputs.shape[0] // req_count
    columns = query_key_value_weight.shape[1]
    kv_local = query_key_value_weight.shape[2]
    requests_per_group = QUERY_HEADS // KEY_VALUE_HEADS
    score_scale = 1.0 / math.sqrt(HEAD_SIZE)
    normalized_input = norm_rows(inputs, attention_gain[0])
    in_weights = query_key_value_weight[0].reshape(
        columns, kv_local * (requests_per_group + 2) * HEAD_SIZE
    )

    def qkv_term(start_row, row_count):
        return jnp.dot(normalized_input, in_weights, preferred_element_type=jnp.float32)

    projected_rows = rows_project(qkv_term, blocks).reshape(
        blocks, kv_local, requests_per_group + 2, HEAD_SIZE
    )
    local_rows = jnp.arange(blocks)
    row_lengths = lengths[0]
    owner_long = (group_index == 0) | (group_index == req_count // 2)
    long_row = (local_rows == 0) & (micro_batch == 0) & owner_long
    position = row_lengths + jnp.where(long_row, LONG, 0).astype(jnp.int32)
    queries = rotate(projected_rows[:, :, :requests_per_group], position).astype(jnp.bfloat16)
    new_key = rotate(projected_rows[:, :, requests_per_group : requests_per_group + 1], position)[
        :, :, 0
    ].astype(jnp.bfloat16)
    new_value = projected_rows[:, :, requests_per_group + 1].astype(jnp.bfloat16)
    gathered = rows_apply(
        queries[0:1].reshape(1, kv_local * requests_per_group * HEAD_SIZE), keep_rows
    )
    long_queries = jnp.stack([gathered[0], gathered[req_count // 2]]).reshape(
        2, kv_local, requests_per_group, HEAD_SIZE
    )
    far_cache = long_cache[0]
    far_live = (jnp.arange(far_cache.shape[1])[None, :] < long_split[:, 0][:, None])[
        :, None, None, :
    ]
    far_scores = (
        jnp.einsum(
            "jkhd,jpkd->jkhp",
            long_queries,
            far_cache[..., :HEAD_SIZE],
            preferred_element_type=jnp.float32,
        )
        * score_scale
    )
    far_max = jnp.max(jnp.where(far_live, far_scores, -jnp.inf), axis=-1)
    far_weights = jnp.where(
        far_live, jnp.exp(jnp.where(far_live, far_scores - far_max[..., None], 0.0)), 0.0
    ).astype(jnp.bfloat16)
    far_totals = jnp.sum(far_weights.astype(jnp.float32), axis=-1)
    far_summed = jnp.einsum(
        "jkhp,jpkd->jkhd",
        far_weights,
        far_cache[..., HEAD_SIZE:],
        preferred_element_type=jnp.float32,
    )
    far_max, far_totals, far_summed = over_requests(
        (far_max, far_totals, far_summed), combine_partial
    )
    far_index = jnp.where(group_index == 0, 0, 1)
    chosen_max = lax.dynamic_index_in_dim(far_max, far_index, 0, keepdims=False)
    chosen_totals = lax.dynamic_index_in_dim(far_totals, far_index, 0, keepdims=False)
    chosen_summed = lax.dynamic_index_in_dim(far_summed, far_index, 0, keepdims=False)
    pack_part = packed_cache[0]
    seg_ends = jnp.cumsum(lengths[0])
    slot_ids = jnp.arange(pack_part.shape[0])
    slot_owner = jnp.sum((slot_ids[:, None] >= seg_ends[None, :]).astype(jnp.int32), axis=1)
    request_ids = micro_batch * blocks + local_rows
    in_segment = (slot_owner[None, :] == request_ids[:, None])[:, None, None, :]
    scores = (
        jnp.einsum(
            "rkhd,pkd->rkhp",
            queries,
            pack_part[..., :HEAD_SIZE],
            preferred_element_type=jnp.float32,
        )
        * score_scale
    )
    own_score = (
        jnp.einsum("rkhd,rkd->rkh", queries, new_key, preferred_element_type=jnp.float32)
        * score_scale
    )
    row_max = jnp.maximum(jnp.max(jnp.where(in_segment, scores, -jnp.inf), axis=-1), own_score)
    long_mask = long_row[:, None, None]
    row_max = jnp.where(long_mask, jnp.maximum(row_max, chosen_max[None]), row_max)
    weights = jnp.where(
        in_segment, jnp.exp(jnp.where(in_segment, scores - row_max[..., None], 0.0)), 0.0
    ).astype(jnp.bfloat16)
    own_weights = jnp.exp(own_score - row_max).astype(jnp.bfloat16)
    far_factor = jnp.where(
        long_mask, jnp.exp(jnp.where(long_mask, chosen_max[None] - row_max, 0.0)), 0.0
    )
    softmax_total = (
        jnp.sum(weights.astype(jnp.float32), axis=-1)
        + own_weights.astype(jnp.float32)
        + far_factor * chosen_totals[None]
    )
    weighted_sum = jnp.einsum(
        "rkhp,pkd->rkhd", weights, pack_part[..., HEAD_SIZE:], preferred_element_type=jnp.float32
    )
    weighted_sum = (
        weighted_sum
        + own_weights.astype(jnp.float32)[..., None] * new_value.astype(jnp.float32)[:, :, None, :]
    )
    weighted_sum = weighted_sum + far_factor[..., None] * chosen_summed[None]
    attended_heads = (
        (weighted_sum / softmax_total[..., None])
        .astype(jnp.bfloat16)
        .reshape(blocks, kv_local * requests_per_group * HEAD_SIZE)
    )
    out_weights = head_output_weight[0].reshape(kv_local * requests_per_group * HEAD_SIZE, columns)

    def project_heads(piece_rows, start_row):
        return jnp.dot(piece_rows, out_weights, preferred_element_type=jnp.float32)

    attended = head_total(rows_apply(attended_heads, project_heads))
    residual = (inputs.astype(jnp.float32) + attended).astype(jnp.bfloat16)
    normed_two = norm_rows(residual, feedforward_gain[0])
    ff_weights = gate_up[0].reshape(columns, -1)

    def ff_term(start_row, row_count):
        return jnp.dot(normed_two, ff_weights, preferred_element_type=jnp.float32)

    gate_and_up = rows_project(ff_term, blocks)
    hidden_width = gate_and_up.shape[1] // 2
    hidden = (jax.nn.silu(gate_and_up[:, :hidden_width]) * gate_and_up[:, hidden_width:]).astype(
        jnp.bfloat16
    )
    lower_weights = down_weight[0]

    def project_hidden(piece_rows, start_row):
        return jnp.dot(piece_rows, lower_weights, preferred_element_type=jnp.float32)

    lowered = head_total(rows_apply(hidden, project_hidden))
    return (residual.astype(jnp.float32) + lowered).astype(jnp.bfloat16)


def local(
    tokens,
    attention_gain,
    query_key_value_weight,
    head_output_weight,
    feedforward_gain,
    gate_up,
    down_weight,
    packed_cache,
    long_cache,
    lengths,
    long_split,
):
    req_count = lax.axis_size("req")
    section_index = lax.axis_index("section")
    batch_count = 1
    per_group = tokens.shape[0] // req_count
    blocks = per_group // batch_count
    columns = tokens.shape[1]
    token_grid = tokens.reshape(req_count, per_group, columns)
    result = jnp.zeros_like(token_grid)
    incoming = jnp.zeros((req_count * blocks, columns), jnp.bfloat16)
    for phase_step in range(batch_count + 1):
        micro_batch = phase_step - section_index
        is_active = (micro_batch >= 0) & (micro_batch < batch_count)
        micro_batch = jnp.clip(micro_batch, 0, batch_count - 1)
        new_batch = token_grid.reshape(req_count * blocks, columns)
        inputs = jnp.where(section_index == 0, new_batch, incoming)
        output = decoder_layer(
            inputs,
            micro_batch,
            attention_gain,
            query_key_value_weight,
            head_output_weight,
            feedforward_gain,
            gate_up,
            down_weight,
            packed_cache,
            long_cache,
            lengths,
            long_split,
        )
        placed = output.reshape(req_count, blocks, columns)
        result = jnp.where(is_active, placed, result)
        if phase_step < batch_count:
            incoming = shifted(output, "section", 1)
    return result.reshape(1, req_count * per_group, columns)


def solution(mesh):
    placed = (
        P(None, "req"),
        P("section", "req"),
        P("section", "req", "head", None),
        P("section", "head", None, "req"),
        P("section", "req"),
        P("section", "req", None, "head"),
        P("section", "head", "req"),
        P("section", "req", "head", None),
        P("section", None, "req", "head", None),
        P("req", None),
        P(None, "req"),
    )
    return jax.shard_map(
        local, mesh=mesh, in_specs=placed, out_specs=P("section", None, "req"), check_vma=False
    )
```

profile of v0, /device:TPU:2, one launch (start us, length us, event | category | flops | bytes accessed | tf_op | source)
XLA Modules:
  0.0 1032.9 jit_solution(9253363095233518662)
XLA Ops:
  6.5 1.2 fusion.34
  7.8 23.3 %all-gather.10 = f32[16,1,256]{2,1,0:T(1,128)S(1)} all-gather(f32[1,1,256]{2,1,0:T(1,128)S(1)} %bitcast.379), channel_id=2, replica_groups=mesh['section'=2,'req'=16,'head'=8] {'req'}, dimensions={0}, use_global_device_ids=true | all-gather | bytes 17408 | tf_op jit(solution)/shard_map/all_gather | solution.py:16
  32.5 3.0 fusion.18
  36.4 78.1 %reduce-scatter.5.cloned.1.call-done = f32[16,1280]{1,0:T(8,128)} async-done(((f32[256,1280]{1,0:T(8,128)}), f32[16,1280]{1,0:T(8,128)}) %reduce-scatter.5.cloned.1.call-update) | async-done | bytes 81936 | tf_op jit(solution)/shard_map/reduce_scatter | solution.py:72
  115.7 21.4 %all-gather.11 = bf16[16,1,1024]{2,1,0:T(2,128)(2,1)S(1)} all-gather(bf16[1,1,1024]{2,1,0:T(2,128)(2,1)S(1)} %reshape.774), channel_id=1, replica_groups=mesh['section'=2,'req'=16,'head'=8] {'req'}, dimensions={0}, use_global_device_ids=true | all-gather | bytes 34816 | tf_op jit(solution)/shard_map/all_gather | solution.py:68
  137.2 1.7 select_reduce_fusion.3
  139.1 1.5 fusion.33
  140.6 22.6 %all-gather.12 = f32[16,2,8]{2,1,0:T(2,128)S(1)} all-gather(f32[1,2,8]{2,1,0:T(2,128)S(1)} %bitcast.371), channel_id=3, replica_groups=mesh['section'=2,'req'=16,'head'=8] {'req'}, dimensions={0}, use_global_device_ids=true | all-gather | bytes 1088 | tf_op jit(solution)/shard_map/all_gather | solution.py:16
  163.2 21.1 %all-gather.13 = f32[16,2,8]{2,1,0:T(2,128)S(1)} all-gather(f32[1,2,8]{2,1,0:T(2,128)S(1)} %bitcast.375), channel_id=4, replica_groups=mesh['section'=2,'req'=16,'head'=8] {'req'}, dimensions={0}, use_global_device_ids=true | all-gather | bytes 1088 | tf_op jit(solution)/shard_map/all_gather | solution.py:16
  184.3 23.0 %all-gather.3 = f32[32,8,128]{2,1,0:T(8,128)S(1)} all-gather(f32[2,8,128]{2,1,0:T(8,128)S(1)} %fusion.33), channel_id=5, replica_groups=mesh['section'=2,'req'=16,'head'=8] {'req'}, dimensions={0}, use_global_device_ids=true | all-gather | bytes 139264 | tf_op jit(solution)/shard_map/all_gather | solution.py:16
  207.4 1.7 while.99
  211.0 21.7 %all_gather.87 = bf16[256,1024]{1,0:T(8,128)(2,1)S(1)} all-gather(bf16[16,1024]{1,0:T(8,128)(2,1)S(1)} %bitcast.340), channel_id=1, replica_groups=mesh['section'=2,'req'=16,'head'=8] {'req'}, dimensions={0}, use_global_device_ids=true | all-gather | bytes 557056 | tf_op jit(solution)/shard_map/all_gather | solution.py:68
  232.7 1.3 fusion.30
  234.1 4.5 copy.75
  238.6 69.5 %all-reduce.5.cloned.1.call-done = f32[256,512]{1,0:T(8,128)} async-done(((f32[256,512]{1,0:T(8,128)}), f32[256,512]{1,0:T(8,128)}) %all-reduce.5.cloned.1.call-update) | async-done | bytes 524304 | tf_op jit(solution)/shard_map/psum | solution.py:81
  308.0 1.2 fusion.38
  309.3 23.0 %all-gather.14 = f32[16,1,256]{2,1,0:T(1,128)S(1)} all-gather(f32[1,1,256]{2,1,0:T(1,128)S(1)} %bitcast.378), channel_id=6, replica_groups=mesh['section'=2,'req'=16,'head'=8] {'req'}, dimensions={0}, use_global_device_ids=true | all-gather | bytes 17408 | tf_op jit(solution)/shard_map/all_gather | solution.py:16
  333.0 5.0 fusion.57
  338.1 77.9 %reduce-scatter.7.cloned.1.call-done = f32[16,3584]{1,0:T(8,128)} async-done(((f32[256,3584]{1,0:T(8,128)}), f32[16,3584]{1,0:T(8,128)}) %reduce-scatter.7.cloned.1.call-update) | async-done | bytes 229392 | tf_op jit(solution)/shard_map/reduce_scatter | solution.py:72
  416.0 1.0 fusion.70
  417.0 23.0 %all_gather.90 = bf16[256,1792]{1,0:T(8,128)(2,1)S(1)} all-gather(bf16[16,1792]{1,0:T(8,128)(2,1)S(1)} %fusion.70), channel_id=1, replica_groups=mesh['section'=2,'req'=16,'head'=8] {'req'}, dimensions={0}, use_global_device_ids=true | all-gather | bytes 974848 | tf_op jit(solution)/shard_map/all_gather | solution.py:68
  440.1 1.4 fusion.14
  441.6 73.4 %all-reduce.7.cloned.1.call-done = f32[256,512]{1,0:T(8,128)} async-done(((f32[256,512]{1,0:T(8,128)}), f32[256,512]{1,0:T(8,128)}) %all-reduce.7.cloned.1.call-update) | async-done | bytes 524304 | tf_op jit(solution)/shard_map/psum | solution.py:81
  515.0 1.9 fusion.41
  516.9 2.0 collective-permute-start
  520.5 23.0 %all-gather.15 = f32[16,1,256]{2,1,0:T(1,128)S(1)} all-gather(f32[1,1,256]{2,1,0:T(1,128)S(1)} %bitcast.376), channel_id=7, replica_groups=mesh['section'=2,'req'=16,'head'=8] {'req'}, dimensions={0}, use_global_device_ids=true | all-gather | bytes 17408 | tf_op jit(solution)/shard_map/all_gather | solution.py:16
  544.2 2.6 fusion.16
  546.8 74.6 %reduce-scatter.9.cloned.1.call-done = f32[16,1280]{1,0:T(8,128)} async-done(((f32[256,1280]{1,0:T(8,128)}), f32[16,1280]{1,0:T(8,128)}) %reduce-scatter.9.cloned.1.call-update) | async-done | bytes 81936 | tf_op jit(solution)/shard_map/reduce_scatter | solution.py:72
  622.6 21.5 %all-gather.16 = bf16[16,1,1024]{2,1,0:T(2,128)(2,1)S(1)} all-gather(bf16[1,1,1024]{2,1,0:T(2,128)(2,1)S(1)} %reshape.784), channel_id=1, replica_groups=mesh['section'=2,'req'=16,'head'=8] {'req'}, dimensions={0}, use_global_device_ids=true | all-gather | bytes 34816 | tf_op jit(solution)/shard_map/all_gather | solution.py:68
  644.1 1.7 select_reduce_fusion.2
  646.0 1.5 fusion.32
  647.7 1.5 select_reduce_fusion
  649.5 22.6 %all-gather.17 = f32[16,2,8]{2,1,0:T(2,128)S(1)} all-gather(f32[1,2,8]{2,1,0:T(2,128)S(1)} %bitcast.370), channel_id=8, replica_groups=mesh['section'=2,'req'=16,'head'=8] {'req'}, dimensions={0}, use_global_device_ids=true | all-gather | bytes 1088 | tf_op jit(solution)/shard_map/all_gather | solution.py:16
  672.1 21.1 %all-gather.18 = f32[16,2,8]{2,1,0:T(2,128)S(1)} all-gather(f32[1,2,8]{2,1,0:T(2,128)S(1)} %bitcast.374), channel_id=9, replica_groups=mesh['section'=2,'req'=16,'head'=8] {'req'}, dimensions={0}, use_global_device_ids=true | all-gather | bytes 1088 | tf_op jit(solution)/shard_map/all_gather | solution.py:16
  693.2 22.9 %all-gather.8 = f32[32,8,128]{2,1,0:T(8,128)S(1)} all-gather(f32[2,8,128]{2,1,0:T(8,128)S(1)} %fusion.32), channel_id=10, replica_groups=mesh['section'=2,'req'=16,'head'=8] {'req'}, dimensions={0}, use_global_device_ids=true | all-gather | bytes 139264 | tf_op jit(solution)/shard_map/all_gather | solution.py:16
  716.1 1.7 while.102
  718.4 1.5 fusion.26
  719.9 22.1 %all_gather.100 = bf16[256,1024]{1,0:T(8,128)(2,1)S(1)} all-gather(bf16[16,1024]{1,0:T(8,128)(2,1)S(1)} %bitcast.341), channel_id=1, replica_groups=mesh['section'=2,'req'=16,'head'=8] {'req'}, dimensions={0}, use_global_device_ids=true | all-gather | bytes 557056 | tf_op jit(solution)/shard_map/all_gather | solution.py:68
  742.0 1.2 fusion.28
  743.4 73.8 %all-reduce.9.cloned.1.call-done = f32[256,512]{1,0:T(8,128)} async-done(((f32[256,512]{1,0:T(8,128)}), f32[256,512]{1,0:T(8,128)}) %all-reduce.9.cloned.1.call-update) | async-done | bytes 524304 | tf_op jit(solution)/shard_map/psum | solution.py:81
  817.2 1.2 fusion.46
  818.4 23.0 %all-gather.19 = f32[16,1,256]{2,1,0:T(1,128)S(1)} all-gather(f32[1,1,256]{2,1,0:T(1,128)S(1)} %bitcast.377), channel_id=11, replica_groups=mesh['section'=2,'req'=16,'head'=8] {'req'}, dimensions={0}, use_global_device_ids=true | all-gather | bytes 17408 | tf_op jit(solution)/shard_map/all_gather | solution.py:16
  842.1 5.0 fusion.54
  847.2 78.0 %reduce-scatter.11.cloned.1.call-done = f32[16,3584]{1,0:T(8,128)} async-done(((f32[256,3584]{1,0:T(8,128)}), f32[16,3584]{1,0:T(8,128)}) %reduce-scatter.11.cloned.1.call-update) | async-done | bytes 229392 | tf_op jit(solution)/shard_map/reduce_scatter | solution.py:72
  926.2 23.0 %all_gather.103 = bf16[256,1792]{1,0:T(8,128)(2,1)S(1)} all-gather(bf16[16,1792]{1,0:T(8,128)(2,1)S(1)} %fusion.69), channel_id=1, replica_groups=mesh['section'=2,'req'=16,'head'=8] {'req'}, dimensions={0}, use_global_device_ids=true | all-gather | bytes 974848 | tf_op jit(solution)/shard_map/all_gather | solution.py:68
  949.2 1.5 fusion.12
  950.7 73.4 %all-reduce.11.cloned.1.call-done = f32[256,512]{1,0:T(8,128)} async-done(((f32[256,512]{1,0:T(8,128)}), f32[256,512]{1,0:T(8,128)}) %all-reduce.11.cloned.1.call-update) | async-done | bytes 524304 | tf_op jit(solution)/shard_map/psum | solution.py:81
  1024.1 1.9 fusion.53
  (354 shorter events, 17.5 us)
Async XLA Ops:
  6.5 433.5 %copy-start = (bf16[1,1792,512]{2,1,0:T(8,128)(2,1)S(1)}, bf16[1,1792,512]{2,1,0:T(8,128)(2,1)}, u32[]{:S(2)}) copy-start(bf16[1,1792,512]{2,1,0:T(8,128)(2,1)} %param.29) | copy-start | bytes 5505028
  6.5 108.0 %reduce-scatter.5.cloned.1.call-start = ((), (), s32[]{:S(2)}) async-start(), calls=%async_computation.4 | async-start | bytes 1392640 | tf_op jit(solution)/shard_map/reduce_scatter | solution.py:72
  32.5 3.2 copy-start.9
  32.5 3.7 copy-start.10
  35.6 272.5 %all-reduce.5.cloned.1.call-start = ((), (), s32[]{:S(2)}) async-start(), calls=%async_computation.5 | async-start | bytes 1048576 | tf_op jit(solution)/shard_map/psum | solution.py:81
  35.9 173.5 %copy-start.7 = (bf16[1,2048,1,256]{3,1,2,0:T(8,128)(2,1)S(1)}, bf16[1,2048,1,256]{3,1,2,0:T(8,128)(2,1)}, u32[]{:S(2)}) copy-start(bf16[1,2048,1,256]{3,1,2,0:T(8,128)(2,1)} %param.30) | copy-start | bytes 3145732
  210.1 22.7 %copy-start.3 = (bf16[1,1,1024,512]{3,2,1,0:T(8,128)(2,1)S(1)}, bf16[1,1,1024,512]{3,2,1,0:T(8,128)(2,1)}, u32[]{:S(2)}) copy-start(bf16[1,1,1024,512]{3,2,1,0:T(8,128)(2,1)} %param.26) | copy-start | bytes 3145732
  234.0 182.0 %reduce-scatter.7.cloned.1.call-start = ((), (), s32[]{:S(2)}) async-start(), calls=%async_computation.6 | async-start | bytes 3899392 | tf_op jit(solution)/shard_map/reduce_scatter | solution.py:72
  234.1 4.5 copy-start.8
  234.1 74.0 %copy-start.2 = (bf16[256,512]{1,0:T(8,128)(2,1)S(1)}, bf16[256,512]{1,0:T(8,128)(2,1)}, u32[]{:S(2)}) copy-start(bf16[256,512]{1,0:T(8,128)(2,1)} %param.23) | copy-start | bytes 786436
  309.3 28.8 %copy-start.5 = (bf16[256,512]{1,0:T(8,128)(2,1)}, bf16[256,512]{1,0:T(8,128)(2,1)S(1)}, u32[]{:S(2)}) copy-start(bf16[256,512]{1,0:T(8,128)(2,1)S(1)} %get-tuple-element.859) | copy-start | bytes 786436
  338.1 176.9 %all-reduce.7.cloned.1.call-start = ((), (), s32[]{:S(2)}) async-start(), calls=%async_computation.7 | async-start | bytes 1048576 | tf_op jit(solution)/shard_map/psum | solution.py:81
  441.5 102.7 %copy-start.1 = (bf16[1,512,1,1280]{3,1,2,0:T(8,128)(2,1)S(1)}, bf16[1,512,1,1280]{3,1,2,0:T(8,128)(2,1)}, u32[]{:S(2)}) copy-start(bf16[1,512,1,1280]{3,1,2,0:T(8,128)(2,1)} %param.25) | copy-start | bytes 3932164
  441.5 179.9 %reduce-scatter.9.cloned.1.call-start = ((), (), s32[]{:S(2)}) async-start(), calls=%async_computation.8 | async-start | bytes 1392640 | tf_op jit(solution)/shard_map/reduce_scatter | solution.py:72
  516.9 2.8 collective-permute-start
  546.8 270.4 %all-reduce.9.cloned.1.call-start = ((), (), s32[]{:S(2)}) async-start(), calls=%async_computation.9 | async-start | bytes 1048576 | tf_op jit(solution)/shard_map/psum | solution.py:81
  717.9 24.1 %copy-start.4 = (bf16[1,1,1024,512]{3,2,1,0:T(8,128)(2,1)S(1)}, bf16[1,1,1024,512]{3,2,1,0:T(8,128)(2,1)}, u32[]{:S(2)}) copy-start(bf16[1,1,1024,512]{3,2,1,0:T(8,128)(2,1)} %param.26) | copy-start | bytes 3145732
  719.9 97.2 %copy-start.6 = (bf16[256,512]{1,0:T(8,128)(2,1)S(1)}, bf16[256,512]{1,0:T(8,128)(2,1)}, u32[]{:S(2)}) copy-start(bf16[256,512]{1,0:T(8,128)(2,1)} %get-tuple-element.857) | copy-start | bytes 786436
  743.3 181.8 %reduce-scatter.11.cloned.1.call-start = ((), (), s32[]{:S(2)}) async-start(), calls=%async_computation.10 | async-start | bytes 3899392 | tf_op jit(solution)/shard_map/reduce_scatter | solution.py:72
  847.2 176.9 %all-reduce.11.cloned.1.call-start = ((), (), s32[]{:S(2)}) async-start(), calls=%async_computation.11 | async-start | bytes 1048576 | tf_op jit(solution)/shard_map/psum | solution.py:81
Sparse Core Ops, SparseCore 0:
  35.7 78.7 reduce-scatter.4
  234.1 73.8 all-reduce.4
  338.2 77.7 reduce-scatter.6
  441.6 73.2 all-reduce.6
  546.9 74.4 reduce-scatter.8
  743.4 73.6 all-reduce.8
  847.3 77.8 reduce-scatter.10
  950.8 73.2 all-reduce.10
where the time goes:
time: 1030 us
  waiting for transfers between devices  600 us (58%)
  blocking collectives  358 us (35%)
  matrix products  31.8 us (3%)
  other arithmetic  17.6 us (2%)
  between operations  13.9 us (1%)
    reduce_scatter x4, waiting for transfers between devices, rows_project(): lax.psum_scatter(term_fn(jnp.int32(0), row_count * lax.axis_size('req')),...  309 us
    psum x4, waiting for transfers between devices, head_total(): return lax.psum(values, 'head')  290 us
    all_gather x10, blocking collectives, merged(): gathered = jax.tree.map(lambda a: lax.all_gather(a, axis), part)  226 us
    all_gather x6, blocking collectives, rows_apply(): lax.all_gather(values, 'req', axis=0, tiled=True)  133 us
  transfers between devices with their start and end apart: 9, of which 9 were waited for; matrix products, arithmetic and copies ran while one was open for 1% of the time, Pallas kernels for 0%

commit v1 on v0

--- a/solution.py
+++ b/solution.py
@@ -78,7 +78,7 @@
 
 
 def head_total(values):
-    return lax.psum(values, "head")
+    return jnp.sum(lax.all_gather(values, "head"), axis=0)
 
 
 def keep_rows(piece_rows, start_row):

time: 1030 us -> 968 us (0.940)
  waiting for transfers between devices: 600 us -> 526 us
    psum x4 -> x0, waiting for transfers between devices: 290 us -> none  [head_total(): return lax.psum(values, 'head')]
    all_gather x0 -> x4, waiting for transfers between devices: none -> 216 us  [head_total(): return jnp.sum(lax.all_gather(values, 'head'), axis=0)]
    reduce_sum x0 -> x4, other arithmetic: none -> 11.7 us  [head_total(): return jnp.sum(lax.all_gather(values, 'head'), axis=0)]
where the time goes in v1:
time: 968 us; the launch traced here: 967 us
  waiting for transfers between devices  526 us (54%)
  blocking collectives  358 us (37%)
  matrix products  29.8 us (3%)
  other arithmetic  27.3 us (3%)
  between operations  13.9 us (1%)
    reduce_scatter x4, waiting for transfers between devices, rows_project(): lax.psum_scatter(term_fn(jnp.int32(0), row_count * lax.axis_size('req')),...  309 us
    all_gather x10, blocking collectives, merged(): gathered = jax.tree.map(lambda a: lax.all_gather(a, axis), part)  226 us
    all_gather x4, waiting for transfers between devices, head_total(): return jnp.sum(lax.all_gather(values, 'head'), axis=0)  216 us
    all_gather x6, blocking collectives, rows_apply(): lax.all_gather(values, 'req', axis=0, tiled=True)  132 us
  transfers between devices with their start and end apart: 9, of which 9 were waited for; matrix products, arithmetic and copies ran while one was open for 1% of the time, Pallas kernels for 0%

profile of v1, /device:TPU:2, one launch (start us, length us, event | category | flops | bytes accessed | tf_op | source)
XLA Modules:
  0.0 966.7 jit_solution(17287327241471967967)
XLA Ops:
  6.5 1.2 fusion.34
  7.8 23.3 %all-gather.14 = f32[16,1,256]{2,1,0:T(1,128)S(1)} all-gather(f32[1,1,256]{2,1,0:T(1,128)S(1)} %bitcast.387), channel_id=2, replica_groups=mesh['section'=2,'req'=16,'head'=8] {'req'}, dimensions={0}, use_global_device_ids=true | all-gather | bytes 17408 | tf_op jit(solution)/shard_map/all_gather | solution.py:16
  32.5 3.1 fusion.18
  36.4 78.1 %reduce-scatter.5.cloned.1.call-done = f32[16,1280]{1,0:T(8,128)} async-done(((f32[256,1280]{1,0:T(8,128)}), f32[16,1280]{1,0:T(8,128)}) %reduce-scatter.5.cloned.1.call-update) | async-done | bytes 81936 | tf_op jit(solution)/shard_map/reduce_scatter | solution.py:72
  115.6 21.4 %all-gather.15 = bf16[16,1,1024]{2,1,0:T(2,128)(2,1)S(1)} all-gather(bf16[1,1,1024]{2,1,0:T(2,128)(2,1)S(1)} %reshape.778), channel_id=1, replica_groups=mesh['section'=2,'req'=16,'head'=8] {'req'}, dimensions={0}, use_global_device_ids=true | all-gather | bytes 34816 | tf_op jit(solution)/shard_map/all_gather | solution.py:68
  137.1 1.7 select_reduce_fusion.3
  138.8 1.5 fusion.33
  140.6 23.0 %all-gather.3 = f32[32,8,128]{2,1,0:T(8,128)S(1)} all-gather(f32[2,8,128]{2,1,0:T(8,128)S(1)} %fusion.33), channel_id=5, replica_groups=mesh['section'=2,'req'=16,'head'=8] {'req'}, dimensions={0}, use_global_device_ids=true | all-gather | bytes 139264 | tf_op jit(solution)/shard_map/all_gather | solution.py:16
  163.6 21.1 %all-gather.17 = f32[16,2,8]{2,1,0:T(2,128)S(1)} all-gather(f32[1,2,8]{2,1,0:T(2,128)S(1)} %bitcast.383), channel_id=4, replica_groups=mesh['section'=2,'req'=16,'head'=8] {'req'}, dimensions={0}, use_global_device_ids=true | all-gather | bytes 1088 | tf_op jit(solution)/shard_map/all_gather | solution.py:16
  184.7 22.6 %all-gather.16 = f32[16,2,8]{2,1,0:T(2,128)S(1)} all-gather(f32[1,2,8]{2,1,0:T(2,128)S(1)} %bitcast.379), channel_id=3, replica_groups=mesh['section'=2,'req'=16,'head'=8] {'req'}, dimensions={0}, use_global_device_ids=true | all-gather | bytes 1088 | tf_op jit(solution)/shard_map/all_gather | solution.py:16
  207.3 1.7 while.99
  210.9 21.8 %all_gather.111 = bf16[256,1024]{1,0:T(8,128)(2,1)S(1)} all-gather(bf16[16,1024]{1,0:T(8,128)(2,1)S(1)} %bitcast.348), channel_id=1, replica_groups=mesh['section'=2,'req'=16,'head'=8] {'req'}, dimensions={0}, use_global_device_ids=true | all-gather | bytes 557056 | tf_op jit(solution)/shard_map/all_gather | solution.py:68
  232.7 1.3 fusion.30
  234.0 4.5 copy.75
  238.5 50.8 %all-gather.29.cloned.1.call-done = f32[2048,512]{1,0:T(8,128)} async-done(((f32[256,512]{1,0:T(8,128)}), f32[2048,512]{1,0:T(8,128)}) %all-gather.29.cloned.1.call-update) | async-done | bytes 4194320 | tf_op jit(solution)/shard_map/all_gather | solution.py:81
  289.3 2.7 reduce_sum.125
  292.2 23.0 %all-gather.18 = f32[16,1,256]{2,1,0:T(1,128)S(1)} all-gather(f32[1,1,256]{2,1,0:T(1,128)S(1)} %bitcast.386), channel_id=7, replica_groups=mesh['section'=2,'req'=16,'head'=8] {'req'}, dimensions={0}, use_global_device_ids=true | all-gather | bytes 17408 | tf_op jit(solution)/shard_map/all_gather | solution.py:16
  316.0 5.0 fusion.57
  321.0 78.1 %reduce-scatter.7.cloned.1.call-done = f32[16,3584]{1,0:T(8,128)} async-done(((f32[256,3584]{1,0:T(8,128)}), f32[16,3584]{1,0:T(8,128)}) %reduce-scatter.7.cloned.1.call-update) | async-done | bytes 229392 | tf_op jit(solution)/shard_map/reduce_scatter | solution.py:72
  399.1 1.0 fusion.70
  400.1 23.0 %all_gather.116 = bf16[256,1792]{1,0:T(8,128)(2,1)S(1)} all-gather(bf16[16,1792]{1,0:T(8,128)(2,1)S(1)} %fusion.70), channel_id=1, replica_groups=mesh['section'=2,'req'=16,'head'=8] {'req'}, dimensions={0}, use_global_device_ids=true | all-gather | bytes 974848 | tf_op jit(solution)/shard_map/all_gather | solution.py:68
  423.2 1.5 fusion.14
  424.7 54.8 %all-gather.31.cloned.1.call-done = f32[2048,512]{1,0:T(8,128)} async-done(((f32[256,512]{1,0:T(8,128)}), f32[2048,512]{1,0:T(8,128)}) %all-gather.31.cloned.1.call-update) | async-done | bytes 4194320 | tf_op jit(solution)/shard_map/all_gather | solution.py:81
  479.5 3.5 reduce_sum.127
  483.0 2.0 fusion.41
  485.0 2.4 collective-permute-start
  489.0 23.0 %all-gather.19 = f32[16,1,256]{2,1,0:T(1,128)S(1)} all-gather(f32[1,1,256]{2,1,0:T(1,128)S(1)} %bitcast.384), channel_id=9, replica_groups=mesh['section'=2,'req'=16,'head'=8] {'req'}, dimensions={0}, use_global_device_ids=true | all-gather | bytes 17408 | tf_op jit(solution)/shard_map/all_gather | solution.py:16
  512.8 2.6 fusion.16
  515.4 74.7 %reduce-scatter.9.cloned.1.call-done = f32[16,1280]{1,0:T(8,128)} async-done(((f32[256,1280]{1,0:T(8,128)}), f32[16,1280]{1,0:T(8,128)}) %reduce-scatter.9.cloned.1.call-update) | async-done | bytes 81936 | tf_op jit(solution)/shard_map/reduce_scatter | solution.py:72
  591.3 21.4 %all-gather.20 = bf16[16,1,1024]{2,1,0:T(2,128)(2,1)S(1)} all-gather(bf16[1,1,1024]{2,1,0:T(2,128)(2,1)S(1)} %reshape.788), channel_id=1, replica_groups=mesh['section'=2,'req'=16,'head'=8] {'req'}, dimensions={0}, use_global_device_ids=true | all-gather | bytes 34816 | tf_op jit(solution)/shard_map/all_gather | solution.py:68
  612.8 1.7 select_reduce_fusion.2
  614.4 1.5 fusion.32
  616.3 23.0 %all-gather.10 = f32[32,8,128]{2,1,0:T(8,128)S(1)} all-gather(f32[2,8,128]{2,1,0:T(8,128)S(1)} %fusion.32), channel_id=12, replica_groups=mesh['section'=2,'req'=16,'head'=8] {'req'}, dimensions={0}, use_global_device_ids=true | all-gather | bytes 139264 | tf_op jit(solution)/shard_map/all_gather | solution.py:16
  639.2 21.1 %all-gather.22 = f32[16,2,8]{2,1,0:T(2,128)S(1)} all-gather(f32[1,2,8]{2,1,0:T(2,128)S(1)} %bitcast.382), channel_id=11, replica_groups=mesh['section'=2,'req'=16,'head'=8] {'req'}, dimensions={0}, use_global_device_ids=true | all-gather | bytes 1088 | tf_op jit(solution)/shard_map/all_gather | solution.py:16
  660.3 22.8 %all-gather.21 = f32[16,2,8]{2,1,0:T(2,128)S(1)} all-gather(f32[1,2,8]{2,1,0:T(2,128)S(1)} %bitcast.378), channel_id=10, replica_groups=mesh['section'=2,'req'=16,'head'=8] {'req'}, dimensions={0}, use_global_device_ids=true | all-gather | bytes 1088 | tf_op jit(solution)/shard_map/all_gather | solution.py:16
  683.1 1.7 while.102
  686.8 21.8 %all_gather.128 = bf16[256,1024]{1,0:T(8,128)(2,1)S(1)} all-gather(bf16[16,1024]{1,0:T(8,128)(2,1)S(1)} %bitcast.349), channel_id=1, replica_groups=mesh['section'=2,'req'=16,'head'=8] {'req'}, dimensions={0}, use_global_device_ids=true | all-gather | bytes 557056 | tf_op jit(solution)/shard_map/all_gather | solution.py:68
  708.5 1.3 fusion.28
  709.9 55.3 %all-gather.33.cloned.1.call-done = f32[2048,512]{1,0:T(8,128)} async-done(((f32[256,512]{1,0:T(8,128)}), f32[2048,512]{1,0:T(8,128)}) %all-gather.33.cloned.1.call-update) | async-done | bytes 4194320 | tf_op jit(solution)/shard_map/all_gather | solution.py:81
  765.2 2.7 reduce_sum.131
  768.1 23.0 %all-gather.23 = f32[16,1,256]{2,1,0:T(1,128)S(1)} all-gather(f32[1,1,256]{2,1,0:T(1,128)S(1)} %bitcast.385), channel_id=14, replica_groups=mesh['section'=2,'req'=16,'head'=8] {'req'}, dimensions={0}, use_global_device_ids=true | all-gather | bytes 17408 | tf_op jit(solution)/shard_map/all_gather | solution.py:16
  791.8 5.0 fusion.54
  796.9 78.1 %reduce-scatter.11.cloned.1.call-done = f32[16,3584]{1,0:T(8,128)} async-done(((f32[256,3584]{1,0:T(8,128)}), f32[16,3584]{1,0:T(8,128)}) %reduce-scatter.11.cloned.1.call-update) | async-done | bytes 229392 | tf_op jit(solution)/shard_map/reduce_scatter | solution.py:72
  876.0 23.1 %all_gather.133 = bf16[256,1792]{1,0:T(8,128)(2,1)S(1)} all-gather(bf16[16,1792]{1,0:T(8,128)(2,1)S(1)} %fusion.69), channel_id=1, replica_groups=mesh['section'=2,'req'=16,'head'=8] {'req'}, dimensions={0}, use_global_device_ids=true | all-gather | bytes 974848 | tf_op jit(solution)/shard_map/all_gather | solution.py:68
  899.0 1.4 fusion.12
  900.5 54.8 %all-gather.35.cloned.1.call-done = f32[2048,512]{1,0:T(8,128)} async-done(((f32[256,512]{1,0:T(8,128)}), f32[2048,512]{1,0:T(8,128)}) %all-gather.35.cloned.1.call-update) | async-done | bytes 4194320 | tf_op jit(solution)/shard_map/all_gather | solution.py:81
  955.3 2.7 reduce_sum.133
  958.0 1.8 fusion.53
  (360 shorter events, 18.9 us)
Async XLA Ops:
  6.5 416.6 %copy-start = (bf16[1,1792,512]{2,1,0:T(8,128)(2,1)S(1)}, bf16[1,1792,512]{2,1,0:T(8,128)(2,1)}, u32[]{:S(2)}) copy-start(bf16[1,1792,512]{2,1,0:T(8,128)(2,1)} %param.29) | copy-start | bytes 5505028
  6.5 108.0 %reduce-scatter.5.cloned.1.call-start = ((), (), s32[]{:S(2)}) async-start(), calls=%async_computation.4 | async-start | bytes 1392640 | tf_op jit(solution)/shard_map/reduce_scatter | solution.py:72
  32.5 3.2 copy-start.10
  32.5 3.7 copy-start.11
  35.6 253.7 %all-gather.29.cloned.1.call-start = ((), (), s32[]{:S(2)}) async-start(), calls=%async_computation.8 | async-start | bytes 4718592 | tf_op jit(solution)/shard_map/all_gather | solution.py:81
  36.1 173.3 %copy-start.7 = (bf16[1,2048,1,256]{3,1,2,0:T(8,128)(2,1)S(1)}, bf16[1,2048,1,256]{3,1,2,0:T(8,128)(2,1)}, u32[]{:S(2)}) copy-start(bf16[1,2048,1,256]{3,1,2,0:T(8,128)(2,1)} %param.30) | copy-start | bytes 3145732
  209.9 22.7 %copy-start.3 = (bf16[1,1,1024,512]{3,2,1,0:T(8,128)(2,1)S(1)}, bf16[1,1,1024,512]{3,2,1,0:T(8,128)(2,1)}, u32[]{:S(2)}) copy-start(bf16[1,1,1024,512]{3,2,1,0:T(8,128)(2,1)} %param.26) | copy-start | bytes 3145732
  234.0 165.1 %reduce-scatter.7.cloned.1.call-start = ((), (), s32[]{:S(2)}) async-start(), calls=%async_computation.5 | async-start | bytes 3899392 | tf_op jit(solution)/shard_map/reduce_scatter | solution.py:72
  234.0 4.5 copy-start.9
  289.3 2.7 copy-start.2
  292.2 28.7 %copy-start.5 = (bf16[256,512]{1,0:T(8,128)(2,1)}, bf16[256,512]{1,0:T(8,128)(2,1)S(1)}, u32[]{:S(2)}) copy-start(bf16[256,512]{1,0:T(8,128)(2,1)S(1)} %get-tuple-element.859) | copy-start | bytes 786436
  321.0 158.5 %all-gather.31.cloned.1.call-start = ((), (), s32[]{:S(2)}) async-start(), calls=%async_computation.9 | async-start | bytes 4718592 | tf_op jit(solution)/shard_map/all_gather | solution.py:81
  424.6 165.5 %reduce-scatter.9.cloned.1.call-start = ((), (), s32[]{:S(2)}) async-start(), calls=%async_computation.6 | async-start | bytes 1392640 | tf_op jit(solution)/shard_map/reduce_scatter | solution.py:72
  483.0 29.8 %copy-start.1 = (bf16[1,512,1,1280]{3,1,2,0:T(8,128)(2,1)S(1)}, bf16[1,512,1,1280]{3,1,2,0:T(8,128)(2,1)}, u32[]{:S(2)}) copy-start(bf16[1,512,1,1280]{3,1,2,0:T(8,128)(2,1)} %param.25) | copy-start | bytes 3932164
  485.0 3.2 collective-permute-start
  515.4 169.8 %copy-start.8 = (bf16[1,2048,1,256]{3,1,2,0:T(8,128)(2,1)S(1)}, bf16[1,2048,1,256]{3,1,2,0:T(8,128)(2,1)}, u32[]{:S(2)}) copy-start(bf16[1,2048,1,256]{3,1,2,0:T(8,128)(2,1)} %param.30) | copy-start | bytes 3145732
  515.4 249.8 %all-gather.33.cloned.1.call-start = ((), (), s32[]{:S(2)}) async-start(), calls=%async_computation.10 | async-start | bytes 4718592 | tf_op jit(solution)/shard_map/all_gather | solution.py:81
  685.8 22.7 %copy-start.4 = (bf16[1,1,1024,512]{3,2,1,0:T(8,128)(2,1)S(1)}, bf16[1,1,1024,512]{3,2,1,0:T(8,128)(2,1)}, u32[]{:S(2)}) copy-start(bf16[1,1,1024,512]{3,2,1,0:T(8,128)(2,1)} %param.26) | copy-start | bytes 3145732
  709.8 165.1 %reduce-scatter.11.cloned.1.call-start = ((), (), s32[]{:S(2)}) async-start(), calls=%async_computation.7 | async-start | bytes 3899392 | tf_op jit(solution)/shard_map/reduce_scatter | solution.py:72
  765.2 2.7 copy-start.6
  796.8 158.5 %all-gather.35.cloned.1.call-start = ((), (), s32[]{:S(2)}) async-start(), calls=%async_computation.11 | async-start | bytes 4718592 | tf_op jit(solution)/shard_map/all_gather | solution.py:81
Sparse Core Ops, SparseCore 0:
  35.7 78.7 reduce-scatter.4
  234.1 55.1 all-gather.28
  321.1 77.9 reduce-scatter.6
  424.8 54.6 all-gather.30
  515.5 74.6 reduce-scatter.8
  710.0 55.1 all-gather.32
  797.0 77.9 reduce-scatter.10
  900.6 54.6 all-gather.34
